TPU v7x, 128 devices: a whole 4x4x4 slice. The times are simulated.
128 devices in a mesh: fsdp: 8 (over x, core), tensor: 2 (over y_lo), context: 8 (over z, y_hi).
Axes of the slice: x: 4, y: 4 (y_hi: 2, y_lo: 2; y = y_hi * 2 + y_lo), z: 4, core: 2. Of those that a mesh axis runs over, the one named last changes fastest.
Arguments:
- block_input: bfloat16 [16384, 768], P(('fsdp', 'context')), may hold values from -6 to 6
- seq_lengths: int32 [8, 3], P('fsdp'), may hold values from 1 to 1536, 2048 in all within a row
- attn_gain: bfloat16 [768], P('fsdp'), may hold values from 0.5 to 1.5
- qkv_weight: bfloat16 [768, 3, 768], P('fsdp', None, 'tensor'), may hold values from -0.3969283 to 0.3969283
- proj_weight: bfloat16 [768, 768], P('tensor', 'fsdp'), may hold values from -4 to 4
- mlp_gain: bfloat16 [768], P('fsdp'), may hold values from 0.5 to 1.5
- gelu_weight: bfloat16 [768, 2, 1152], P('fsdp', None, 'tensor'), may hold values from -0.21875 to 0.21875
- down_weight: bfloat16 [1152, 768], P('tensor', 'fsdp'), may hold values from -0.1875 to 0.1875
- out_cotangent: bfloat16 [16384, 768], P(('fsdp', 'context')), may hold values from -6 to 6
Outputs:
- block_output: bfloat16 [16384, 768], P(('fsdp', 'context'))
- input_grad: float32 [16384, 768], P(('fsdp', 'context'))
- attngain_grad: float32 [768], P('fsdp')
- qkv_grad: float32 [768, 3, 768], P('fsdp', None, 'tensor')
- proj_grad: float32 [768, 768], P('tensor', 'fsdp')
- mlpgain_grad: float32 [768], P('fsdp')
- gelu_grad: float32 [768, 2, 1152], P('fsdp', None, 'tensor')
- down_grad: float32 [1152, 768], P('tensor', 'fsdp')
All inputs are finite; a program needn't handle non-finite values.
Results may differ from a plain program's by a relative error of at most 0.02.
Values may be sent and summed in bfloat16 or wider, within the bound.
A program may use at most 128 MiB of HBM per device.

v0:
```python
import jax
import jax.numpy as jnp
from jax import lax
from jax.sharding import PartitionSpec as P

HD = 64
EPSILON = 1e-05
THETA = 160000.0
MASKED_LOW = -1e30


def layer_norm(values):
    centre = values - jnp.mean(values, axis=-1, keepdims=True)
    spread = lax.rsqrt(jnp.mean(centre * centre, axis=-1, keepdims=True) + EPSILON)
    return (centre * spread, spread)


def norm_back(grad_out, normed, spread, gain):
    scaled = grad_out * gain
    inner = jnp.mean(scaled, axis=-1, keepdims=True) + normed * jnp.mean(
        scaled * normed, axis=-1, keepdims=True
    )
    return spread * (scaled - inner)


def segments_of(row_ids, lengths):
    ends = jnp.cumsum(lengths)
    segment = jnp.sum((row_ids[:, None] >= ends[None, :]).astype(jnp.int32), axis=1)
    starts = ends - lengths
    picked = segment[:, None] == jnp.arange(lengths.shape[0], dtype=jnp.int32)[None, :]
    begin = jnp.sum(jnp.where(picked, starts[None, :], 0), axis=1)
    return (segment, row_ids - begin)


def rope_tables(positions, head_dim):
    half_dim = head_dim // 2
    exponent = jnp.arange(half_dim, dtype=jnp.float32) * (-2.0 / head_dim)
    frequency = jnp.power(jnp.float32(THETA), exponent)
    angles = positions.astype(jnp.float32)[:, None] * frequency[None, :]
    return (jnp.cos(angles)[:, None, :], jnp.sin(angles)[:, None, :])


def rotate(values, cosine, sine_tab):
    half_dim = values.shape[-1] // 2
    lower_half, upper_half = (values[..., :half_dim], values[..., half_dim:])
    return jnp.concatenate(
        [lower_half * cosine - upper_half * sine_tab, upper_half * cosine + lower_half * sine_tab],
        axis=-1,
    )


def rotate_back(grads, cosine, sine_tab):
    half_dim = grads.shape[-1] // 2
    lower_half, upper_half = (grads[..., :half_dim], grads[..., half_dim:])
    return jnp.concatenate(
        [lower_half * cosine + upper_half * sine_tab, upper_half * cosine - lower_half * sine_tab],
        axis=-1,
    )


def gelu_parts(gate_pre):
    normal_cdf = 0.5 * (1.0 + jax.scipy.special.erf(gate_pre * 0.7071067811865476))
    density = jnp.exp(-0.5 * gate_pre * gate_pre) * 0.3989422804014327
    return (gate_pre * normal_cdf, normal_cdf + gate_pre * density)


def split_count(row_count):
    pieces = 1
    while row_count // pieces > 1024 and row_count % (2 * pieces) == 0:
        pieces = pieces * 2
    return pieces


def over_blocks(step, running, members):
    row_count = members[0].shape[0]
    pieces = split_count(row_count)
    stride = row_count // pieces

    def one_block(counter, current):
        offset = counter * stride
        sliced = tuple((lax.dynamic_slice_in_dim(member, offset, stride, 0) for member in members))
        return step(current, sliced, offset)

    return lax.fori_loop(0, pieces, one_block, running)


def guarded(step):

    def wrapped(running, members, first_row):
        return step(running, members, first_row)

    def folded(running, members, first_row):
        return over_blocks(wrapped, running, members)

    return folded


def on_device(
    block_input,
    seq_lengths,
    attn_gain,
    qkv_weight,
    proj_weight,
    mlp_gain,
    gelu_weight,
    down_weight,
    out_cotangent,
):
    row_count = block_input.shape[0]
    feature_count = block_input.shape[1]
    lengths = seq_lengths[0]
    group_rows = row_count * lax.axis_size("context")
    own_first = lax.axis_index("context") * row_count
    own_rows = own_first + jnp.arange(row_count, dtype=jnp.int32)
    own_segment, positions = segments_of(own_rows, lengths)
    cosine, sine_tab = rope_tables(positions, HD)
    gathered = (
        lax.all_gather(qkv_weight, "fsdp", axis=0, tiled=True),
        lax.all_gather(proj_weight, "fsdp", axis=1, tiled=True),
        lax.all_gather(gelu_weight, "fsdp", axis=0, tiled=True),
        lax.all_gather(down_weight, "fsdp", axis=1, tiled=True),
        lax.all_gather(attn_gain, "fsdp", axis=0, tiled=True),
        lax.all_gather(mlp_gain, "fsdp", axis=0, tiled=True),
    )
    qkv_full, proj_full, gelu_full, down_full, attn_full, mlp_full = gathered
    local_width = qkv_full.shape[2]
    head_count = local_width // HD
    hidden = gelu_full.shape[2]
    attn_scale = attn_full.astype(jnp.float32)
    mlp_scale = mlp_full.astype(jnp.float32)
    inputs = block_input.astype(jnp.float32)
    normed_attn, spread_attn = layer_norm(inputs)
    hidden_attn = (normed_attn * attn_scale).astype(jnp.bfloat16)
    qkv_flat = qkv_full.reshape(feature_count, 3 * local_width)
    projected = jnp.dot(hidden_attn, qkv_flat, preferred_element_type=jnp.float32).reshape(
        row_count, 3, head_count, HD
    )
    query_bf = rotate(projected[:, 0], cosine, sine_tab).astype(jnp.bfloat16)
    key_bf = rotate(projected[:, 1], cosine, sine_tab).astype(jnp.bfloat16)
    value_bf = projected[:, 2].astype(jnp.bfloat16)
    key_flat = key_bf.reshape(row_count, local_width)
    value_flat = value_bf.reshape(row_count, local_width)
    keys_group, values_group = (
        lax.all_gather(key_flat, "context", axis=0, tiled=True),
        lax.all_gather(value_flat, "context", axis=0, tiled=True),
    )
    keys_heads = keys_group.reshape(group_rows, head_count, HD)
    values_heads = values_group.reshape(group_rows, head_count, HD)
    group_segment, unused_pos = segments_of(jnp.arange(group_rows, dtype=jnp.int32), lengths)
    same_group = (own_segment[:, None] == group_segment[None, :])[None]
    fwd_scores = (
        jnp.einsum("qhd,khd->hqk", query_bf, keys_heads, preferred_element_type=jnp.float32) * 0.125
    )
    row_max = jnp.max(jnp.where(same_group, fwd_scores, MASKED_LOW), axis=2)
    denom_sum = jnp.sum(
        jnp.where(same_group, jnp.exp(fwd_scores - row_max[:, :, None]), 0.0), axis=2
    )
    log_total = row_max + jnp.log(denom_sum)
    fwd_weights = jnp.where(same_group, jnp.exp(fwd_scores - log_total[:, :, None]), 0.0).astype(
        jnp.bfloat16
    )
    mixed = jnp.einsum(
        "hqk,khd->qhd", fwd_weights, values_heads, preferred_element_type=jnp.float32
    ).astype(jnp.bfloat16)
    mixed_flat = mixed.reshape(row_count, local_width)
    attn_part = jnp.dot(mixed_flat, proj_full, preferred_element_type=jnp.float32)
    residual = inputs + lax.psum(attn_part, "tensor")
    normed_mlp, spread_mlp = layer_norm(residual)
    hidden_mlp = (normed_mlp * mlp_scale).astype(jnp.bfloat16)
    gelu_flat = gelu_full.reshape(feature_count, 2 * hidden)
    gate_up = jnp.dot(hidden_mlp, gelu_flat, preferred_element_type=jnp.float32).reshape(
        row_count, 2, hidden
    )
    gate_pre, up_pre = (gate_up[:, 0], gate_up[:, 1])
    gelu_val, gelu_slope = gelu_parts(gate_pre)
    activ = (gelu_val * up_pre).astype(jnp.bfloat16)
    mlp_part = jnp.dot(activ, down_full, preferred_element_type=jnp.float32)
    block_output = (
        residual + lax.psum(mlp_part.astype(jnp.bfloat16), "tensor").astype(jnp.float32)
    ).astype(jnp.bfloat16)
    act_grad = jnp.dot(out_cotangent, down_full.T, preferred_element_type=jnp.float32)
    down_grad_t = jnp.dot(out_cotangent.T, activ, preferred_element_type=jnp.float32)
    gate_up_grad = (
        jnp.stack([act_grad * up_pre * gelu_slope, act_grad * gelu_val], axis=1)
        .astype(jnp.bfloat16)
        .reshape(row_count, 2 * hidden)
    )
    gelu_grad = jnp.dot(hidden_mlp.T, gate_up_grad, preferred_element_type=jnp.float32).reshape(
        feature_count, 2, hidden
    )
    mlp_in_grad = lax.psum(
        jnp.dot(gate_up_grad, gelu_flat.T, preferred_element_type=jnp.float32), "tensor"
    )
    mlpgain_grad = jnp.sum(mlp_in_grad * normed_mlp, axis=0)
    resid_grad = out_cotangent.astype(jnp.float32) + norm_back(
        mlp_in_grad, normed_mlp, spread_mlp, mlp_scale
    )
    resid_bf = resid_grad.astype(jnp.bfloat16)
    out_grad = jnp.dot(resid_bf, proj_full.T, preferred_element_type=jnp.float32).astype(
        jnp.bfloat16
    )
    proj_grad_t = jnp.dot(resid_bf.T, mixed_flat, preferred_element_type=jnp.float32)
    out_heads = out_grad.reshape(row_count, head_count, HD)
    delta = jnp.transpose(
        jnp.sum(out_heads.astype(jnp.float32) * mixed.astype(jnp.float32), axis=2)
    )

    def key_terms(members, first_row):
        key_count = members[0].shape[0]
        key_part = members[0].reshape(key_count, head_count, HD)
        value_part = members[1].reshape(key_count, head_count, HD)
        key_segment, unused = segments_of(
            first_row + jnp.arange(key_count, dtype=jnp.int32), lengths
        )
        same_doc = (own_segment[:, None] == key_segment[None, :])[None]
        scores = (
            jnp.einsum("qhd,khd->hqk", query_bf, key_part, preferred_element_type=jnp.float32)
            * 0.125
        )
        weights = jnp.where(same_doc, jnp.exp(scores - log_total[:, :, None]), 0.0)
        prob_grad = jnp.einsum(
            "qhd,khd->hqk", out_heads, value_part, preferred_element_type=jnp.float32
        )
        score_grad = (weights * (prob_grad - delta[:, :, None])).astype(jnp.bfloat16)
        return (key_part, weights, score_grad)

    def owner_step(running, members, first_row):
        query_grad, key_all, value_all = running
        key_part, weights, score_grad = key_terms(members, first_row)
        key_count = key_part.shape[0]
        query_grad = (
            query_grad
            + jnp.einsum("hqk,khd->qhd", score_grad, key_part, preferred_element_type=jnp.float32)
            * 0.125
        )
        key_piece = (
            jnp.einsum(
                "hqk,qhd->khd", score_grad, query_bf, preferred_element_type=jnp.float32
            ).reshape(key_count, local_width)
            * 0.125
        )
        value_piece = jnp.einsum(
            "hqk,qhd->khd",
            weights.astype(jnp.bfloat16),
            out_heads,
            preferred_element_type=jnp.float32,
        ).reshape(key_count, local_width)
        key_all = lax.dynamic_update_slice_in_dim(
            key_all,
            lax.dynamic_slice_in_dim(key_all, first_row, key_count, 0) + key_piece,
            first_row,
            0,
        )
        value_all = lax.dynamic_update_slice_in_dim(
            value_all,
            lax.dynamic_slice_in_dim(value_all, first_row, key_count, 0) + value_piece,
            first_row,
            0,
        )
        return (query_grad, key_all, value_all)

    grad_start = jnp.zeros((row_count, head_count, HD), jnp.float32)
    back_state = (
        grad_start,
        jnp.zeros((group_rows, local_width), jnp.float32),
        jnp.zeros((group_rows, local_width), jnp.float32),
    )
    back_result = guarded(owner_step)(
        back_state,
        (
            lax.all_gather(key_flat, "context", axis=0, tiled=True),
            lax.all_gather(value_flat, "context", axis=0, tiled=True),
        ),
        jnp.int32(0),
    )
    query_grad = back_result[0]
    key_grad, value_grad = (
        lax.psum_scatter(
            back_result[1].astype(jnp.bfloat16), "context", scatter_dimension=0, tiled=True
        ).astype(jnp.float32),
        lax.psum_scatter(
            back_result[2].astype(jnp.bfloat16), "context", scatter_dimension=0, tiled=True
        ).astype(jnp.float32),
    )
    key_grad = key_grad.reshape(row_count, head_count, HD)
    value_grad = value_grad.reshape(row_count, head_count, HD)
    qkv_rows = (
        jnp.stack(
            [
                rotate_back(query_grad, cosine, sine_tab),
                rotate_back(key_grad, cosine, sine_tab),
                value_grad,
            ],
            axis=1,
        )
        .astype(jnp.bfloat16)
        .reshape(row_count, 3 * local_width)
    )
    qkv_grad = jnp.dot(hidden_attn.T, qkv_rows, preferred_element_type=jnp.float32).reshape(
        feature_count, 3, local_width
    )
    attn_in_grad = lax.psum(
        jnp.dot(qkv_rows, qkv_flat.T, preferred_element_type=jnp.float32).astype(jnp.bfloat16),
        "tensor",
    ).astype(jnp.float32)
    attngain_grad = jnp.sum(attn_in_grad * normed_attn, axis=0)
    input_grad = resid_grad + norm_back(attn_in_grad, normed_attn, spread_attn, attn_scale)
    grads = (
        attngain_grad[:, None],
        mlpgain_grad[:, None],
        qkv_grad.reshape(feature_count, 3 * local_width),
        gelu_grad.reshape(feature_count, 2 * hidden),
        proj_grad_t,
        down_grad_t,
    )
    widths = [g.shape[1] for g in grads]
    packed = jnp.concatenate(grads, axis=1)
    packed = lax.psum_scatter(packed, "fsdp", scatter_dimension=0, tiled=True)
    packed = lax.psum(packed, "context")
    pieces = []
    start = 0
    for width in widths:
        pieces.append(packed[:, start : start + width])
        start += width
    shard_rows = packed.shape[0]
    shares = (
        pieces[0][:, 0],
        pieces[2].reshape(shard_rows, 3, local_width),
        pieces[4].T,
        pieces[1][:, 0],
        pieces[3].reshape(shard_rows, 2, hidden),
        pieces[5].T,
    )
    return (
        block_output,
        input_grad,
        shares[0],
        shares[1],
        shares[2],
        shares[3],
        shares[4],
        shares[5],
    )


def solution(mesh):
    in_specs = (
        P(("fsdp", "context"), None),
        P("fsdp", None),
        P("fsdp"),
        P("fsdp", None, "tensor"),
        P("tensor", "fsdp"),
        P("fsdp"),
        P("fsdp", None, "tensor"),
        P("tensor", "fsdp"),
        P(("fsdp", "context"), None),
    )
    out_specs = (
        P(("fsdp", "context"), None),
        P(("fsdp", "context"), None),
        P("fsdp"),
        P("fsdp", None, "tensor"),
        P("tensor", "fsdp"),
        P("fsdp"),
        P("fsdp", None, "tensor"),
        P("tensor", "fsdp"),
    )
    return jax.shard_map(
        on_device, mesh=mesh, in_specs=in_specs, out_specs=out_specs, check_vma=False
    )
```

profile of v0, /device:TPU:0, one launch (start us, length us, event | category | flops | bytes accessed | tf_op | source)
XLA Modules:
  0.0 698.4 jit_solution(5407401806397029626)
XLA Ops:
  11.6 14.7 %all-reduce.2 = (bf16[768]{0:T(1024)(128)(2,1)S(1)}, bf16[768]{0:T(1024)(128)(2,1)S(1)}) all-reduce(bf16[768]{0:T(1024)(128)(2,1)S(1)} %dynamic-update-slice, bf16[768]{0:T(1024)(128)(2,1)S(1)} %dynamic-update-slice.1), channel_id=1, replica_groups=mesh['fsdp'=8,'tensor'=2,'context'=8] {'fsdp'}, use_global_device_ids=true, to_apply=%add | all-reduce | flops 1536 | bytes 6144
  30.6 6.5 all-gather.5.cloned.1.call-done
  45.6 13.2 %all_gather.30 = bf16[384,768]{0,1:T(8,128)(2,1)S(1)} all-gather(bf16[384,96]{0,1:T(8,128)(2,1)S(1)} %copy-done.46), channel_id=1, replica_groups=mesh['fsdp'=8,'tensor'=2,'context'=8] {'fsdp'}, dimensions={1}, use_global_device_ids=true | all-gather | bytes 663552 | tf_op jit(solution)/shard_map/all_gather | solution.py:119
  58.8 33.9 %all-gather.9.cloned.1.call-done = bf16[2048,384]{0,1:T(8,128)(2,1)} async-done(((bf16[256,384]{0,1:T(8,128)(2,1)}), bf16[2048,384]{0,1:T(8,128)(2,1)}) %all-gather.9.cloned.1.call-update) | async-done | bytes 1572880 | tf_op jit(solution)/shard_map/all_gather | solution.py:144
  92.7 3.9 select_reduce_fusion.1
  96.6 3.9 select_reduce_fusion
  101.1 42.2 %all-gather.7.cloned.1.call-done = bf16[2048,384]{0,1:T(8,128)(2,1)} async-done(((bf16[256,384]{0,1:T(8,128)(2,1)}), bf16[2048,384]{0,1:T(8,128)(2,1)}) %all-gather.7.cloned.1.call-update) | async-done | bytes 1572880 | tf_op jit(solution)/shard_map/all_gather | solution.py:145
  143.3 7.7 %fusion.13 = bf16[6,64,256]{2,1,0:T(8,128)(2,1)S(1)} fusion(bf16[2048,6,64]{0,2,1:T(8,128)(2,1)} %bitcast.184, f32[6,256,2048]{2,1,0:T(8,128)} %copy-done.7, f32[6,256]{1,0:T(8,128)S(1)} %log_add_fusion, pred[256,2048]{1,0:T(8,128)(4,1)S(1)} %broadcast_compare_fusion.1), kind=kOutput, calls=%fused_computation.37 | convolution fusion | flops 415334400 | bytes 14882816 | tf_op jit(solution)/shard_map/hqk,khd->qhd/dot_general | solution.py:162
  152.4 16.8 %all_gather.33 = bf16[576,768]{0,1:T(8,128)(2,1)} all-gather(bf16[576,96]{0,1:T(8,128)(2,1)S(1)} %copy-done.45), channel_id=1, replica_groups=mesh['fsdp'=8,'tensor'=2,'context'=8] {'fsdp'}, dimensions={1}, use_global_device_ids=true | all-gather | bytes 995328 | tf_op jit(solution)/shard_map/all_gather | solution.py:121
  172.7 40.8 %all-reduce.9.cloned.1.call-done = f32[256,768]{1,0:T(8,128)} async-done(((f32[256,768]{1,0:T(8,128)}), f32[256,768]{1,0:T(8,128)}) %all-reduce.9.cloned.1.call-update) | async-done | bytes 786448 | tf_op jit(solution)/shard_map/psum | solution.py:167
  219.8 41.8 %all-reduce.11.cloned.1.call-done = f32[256,768]{1,0:T(8,128)} async-done(((f32[256,768]{1,0:T(8,128)}), f32[256,768]{1,0:T(8,128)}) %all-reduce.11.cloned.1.call-update) | async-done | bytes 786448 | tf_op jit(solution)/shard_map/psum | solution.py:191
  270.5 40.4 %while.20 = (s32[]{:T(128)}, f32[256,6,64]{0,2,1:T(8,128)}, f32[2048,384]{0,1:T(8,128)}, f32[2048,384]{0,1:T(8,128)}, bf16[2048,384]{0,1:T(8,128)(2,1)}, /*index...) while((s32[]{:T(128)}, f32[256,6,64]{0,2,1:T(8,128)}, ...), condition=%wide.region_19.20_spmd.clone, body=%wide.region_17.19_spmd.clone.sunk | while | flops 1024107520 | bytes 131182336 | solution.py:84
  275.0 3.3 fusion.105
  281.0 4.3 fusion.107
  295.2 3.3 fusion.105
  301.2 4.3 fusion.107
  310.9 3.4 convert_element_type.160
  321.6 67.5 %reduce-scatter.4.cloned.1.call-done = bf16[256,384]{0,1:T(8,128)(2,1)} async-done(((bf16[2048,384]{0,1:T(8,128)(2,1)}), bf16[256,384]{0,1:T(8,128)(2,1)}) %reduce-scatter.4.cloned.1.call-update) | async-done | bytes 196624 | tf_op jit(solution)/shard_map/reduce_scatter | solution.py:278
  391.1 74.7 %reduce-scatter.6.cloned.1.call-done = bf16[256,384]{0,1:T(8,128)(2,1)} async-done(((bf16[2048,384]{0,1:T(8,128)(2,1)}), bf16[256,384]{0,1:T(8,128)(2,1)}) %reduce-scatter.6.cloned.1.call-update) | async-done | bytes 196624 | tf_op jit(solution)/shard_map/reduce_scatter | solution.py:281
  469.1 3.0 convolution_bitcast_fusion
  476.3 32.8 %all-reduce.15.cloned.1.call-done = (bf16[256,768]{1,0:T(8,128)(2,1)}, bf16[256,768]{1,0:T(8,128)(2,1)}) async-done(((bf16[256,768]{1,0:T(8,128)(2,1)}, bf16[256,768]{1,0:T(8,128)(2,1)}), (bf16[256,768]{1,0:T(8,128)(2,1)}, bf16[256,768]{1,0:T(8,128)(2,1)})) %all-reduce.15.cloned.1.call-update) | async-done | bytes 786448 | tf_op jit(solution)/shard_map/psum | solution.py:179
  510.7 13.5 %concatenate.21 = f32[768,3266]{1,0:T(8,128)} concatenate(f32[768,1]{1,0:T(8,128)S(1)} %broadcast_in_dim.141, f32[768,1]{1,0:T(8,128)S(1)} %broadcast_in_dim.142, f32[768,1152]{1,0:T(8,128)} %fusion.45, f32[768,1152]{1,0:T(8,128)} %fusion.48, f32[768,384]{1,0:T(8,128)} %fusion.38, f32[768,576]{1,0:T(8,128)} %convolution_bitcast_fusion), dimensions={1} | concatenate | bytes 20066304 | tf_op jit(solution)/shard_map/concatenate | solution.py:317
  524.3 62.2 %reduce-scatter.8.cloned.1.call-done = f32[96,3266]{1,0:T(8,128)} async-done(((f32[768,3266]{1,0:T(8,128)}), f32[96,3266]{1,0:T(8,128)}) %reduce-scatter.8.cloned.1.call-update) | async-done | bytes 1254160 | tf_op jit(solution)/shard_map/reduce_scatter | solution.py:318
  588.6 94.9 %all-reduce.13.cloned.1.call-done = f32[96,3266]{1,0:T(8,128)} async-done(((f32[96,3266]{1,0:T(8,128)}), f32[96,3266]{1,0:T(8,128)}) %all-reduce.13.cloned.1.call-update) | async-done | bytes 1254160 | tf_op jit(solution)/shard_map/psum | solution.py:319
  (272 shorter events, 90.4 us)
Async XLA Ops:
  7.2 29.9 %all-gather.5.cloned.1.call-start = ((), (), s32[]{:S(2)}) async-start(), calls=%async_computation.3 | async-start | bytes 1990656 | tf_op jit(solution)/shard_map/all_gather | solution.py:118
  7.9 84.8 %all-gather.9.cloned.1.call-start = ((), (), s32[]{:S(2)}) async-start(), calls=%async_computation.5 | async-start | bytes 1769472 | tf_op jit(solution)/shard_map/all_gather | solution.py:144
  41.8 54.8 %copy-start.33 = (bf16[256,6,32]{0,2,1:T(8,128)(2,1)}, bf16[256,6,32]{0,2,1:T(8,128)(2,1)S(1)}, u32[]{:S(2)}) copy-start(bf16[256,6,32]{0,2,1:T(8,128)(2,1)S(1)} %get-tuple-element.409) | copy-start | bytes 294916
  41.8 54.8 %copy-start.35 = (bf16[256,6,32]{0,2,1:T(8,128)(2,1)}, bf16[256,6,32]{0,2,1:T(8,128)(2,1)S(1)}, u32[]{:S(2)}) copy-start(bf16[256,6,32]{0,2,1:T(8,128)(2,1)S(1)} %get-tuple-element.410) | copy-start | bytes 294916
  42.5 100.8 %all-gather.7.cloned.1.call-start = ((), (), s32[]{:S(2)}) async-start(), calls=%async_computation.4 | async-start | bytes 1769472 | tf_op jit(solution)/shard_map/all_gather | solution.py:145
  44.3 125.7 %all-gather.11.cloned.1.call-start = ((), (), s32[]{:S(2)}) async-start(), calls=%async_computation.7 | async-start | bytes 2211840 | tf_op jit(solution)/shard_map/all_gather | solution.py:120
  45.1 168.4 %all-reduce.9.cloned.1.call-start = ((), (), s32[]{:S(2)}) async-start(), calls=%async_computation.6 | async-start | bytes 1572864 | tf_op jit(solution)/shard_map/psum | solution.py:167
  58.8 92.1 %copy-start.19 = (bf16[384,768]{0,1:T(8,128)(2,1)}, bf16[384,768]{0,1:T(8,128)(2,1)S(1)}, u32[]{:S(2)}) copy-start(bf16[384,768]{0,1:T(8,128)(2,1)S(1)} %all_gather.30) | copy-start | bytes 1769476
  101.1 49.8 %copy-start.58 = (f32[6,256]{1,0:T(8,128)}, f32[6,256]{1,0:T(8,128)S(1)}, u32[]{:S(2)}) copy-start(f32[6,256]{1,0:T(8,128)S(1)} %log_add_fusion) | copy-start | bytes 18436
  152.3 109.3 %all-reduce.11.cloned.1.call-start = ((), (), s32[]{:S(2)}) async-start(), calls=%async_computation.8 | async-start | bytes 1572864 | tf_op jit(solution)/shard_map/psum | solution.py:191
  214.9 48.9 %copy-start.8 = (f32[256,768]{1,0:T(8,128)}, f32[256,768]{1,0:T(8,128)S(1)}, u32[]{:S(2)}) copy-start(f32[256,768]{1,0:T(8,128)S(1)} %get-tuple-element.396) | copy-start | bytes 2359300
  217.5 46.2 %copy-start.42 = (bf16[256,1,576]{0,2,1:T(8,128)(2,1)}, bf16[256,1,576]{0,2,1:T(8,128)(2,1)S(1)}, u32[]{:S(2)}) copy-start(bf16[256,1,576]{0,2,1:T(8,128)(2,1)S(1)} %get-tuple-element.399) | copy-start | bytes 884740
  217.5 46.2 %copy-start.43 = (bf16[256,1,576]{0,2,1:T(8,128)(2,1)}, bf16[256,1,576]{0,2,1:T(8,128)(2,1)S(1)}, u32[]{:S(2)}) copy-start(bf16[256,1,576]{0,2,1:T(8,128)(2,1)S(1)} %get-tuple-element.400) | copy-start | bytes 884740
  217.8 45.9 %copy-start.32 = (bf16[256,768]{1,0:T(8,128)(2,1)S(1)}, bf16[256,768]{1,0:T(8,128)(2,1)}, u32[]{:S(2)}) copy-start(bf16[256,768]{1,0:T(8,128)(2,1)} %param.19) | copy-start | bytes 1179652
  219.6 45.6 %copy-start.20 = (bf16[384,768]{0,1:T(8,128)(2,1)S(1)}, bf16[384,768]{0,1:T(8,128)(2,1)}, u32[]{:S(2)}) copy-start(bf16[384,768]{0,1:T(8,128)(2,1)} %copy-done.19) | copy-start | bytes 1769476
  219.6 169.6 %reduce-scatter.4.cloned.1.call-start = ((), (), s32[]{:S(2)}) async-start(), calls=%async_computation.9 | async-start | bytes 1769472 | tf_op jit(solution)/shard_map/reduce_scatter | solution.py:278
  314.4 151.4 %reduce-scatter.6.cloned.1.call-start = ((), (), s32[]{:S(2)}) async-start(), calls=%async_computation.10 | async-start | bytes 1769472 | tf_op jit(solution)/shard_map/reduce_scatter | solution.py:281
  315.9 193.2 %all-reduce.15.cloned.1.call-start = ((), (), s32[]{:S(2)}) async-start(), calls=%async_computation.13 | async-start | bytes 1572864 | tf_op jit(solution)/shard_map/psum | solution.py:179
  318.9 71.2 %copy-start.14 = (f32[256,6,64]{0,2,1:T(8,128)S(1)}, f32[256,6,64]{0,2,1:T(8,128)}, u32[]{:S(2)}) copy-start(f32[256,6,64]{0,2,1:T(8,128)} %get-tuple-element.285) | copy-start | bytes 1179652
  318.9 148.7 %copy-start.13 = (bf16[768,3,384]{0,2,1:T(8,128)(2,1)S(1)}, bf16[768,3,384]{0,2,1:T(8,128)(2,1)}, u32[]{:S(2)}) copy-start(bf16[768,3,384]{0,2,1:T(8,128)(2,1)} %copy-done.12) | copy-start | bytes 5308420
  469.1 117.4 %reduce-scatter.8.cloned.1.call-start = ((), (), s32[]{:S(2)}) async-start(), calls=%async_computation.11 | async-start | bytes 11501568 | tf_op jit(solution)/shard_map/reduce_scatter | solution.py:318
  524.2 62.3 %copy-start.39 = (bf16[256,768]{1,0:T(8,128)(2,1)S(1)}, bf16[256,768]{1,0:T(8,128)(2,1)}, u32[]{:S(2)}) copy-start(bf16[256,768]{1,0:T(8,128)(2,1)} %get-tuple-element.393) | copy-start | bytes 1179652
  524.2 63.2 %copy-start.30 = (bf16[256,768]{1,0:T(8,128)(2,1)S(1)}, bf16[256,768]{1,0:T(8,128)(2,1)}, u32[]{:S(2)}) copy-start(bf16[256,768]{1,0:T(8,128)(2,1)} %get-tuple-element.394) | copy-start | bytes 1179652
  524.3 159.2 %all-reduce.13.cloned.1.call-start = ((), (), s32[]{:S(2)}) async-start(), calls=%async_computation.12 | async-start | bytes 2555904 | tf_op jit(solution)/shard_map/psum | solution.py:319
  (65 other events, 380.2 us)
Sparse Core Ops, SparseCore 0:
  9.7 27.3 all-gather.4
  42.7 50.0 all-gather.8
  95.5 47.7 all-gather.6
  145.4 24.5 all-gather.10
  172.8 40.5 all-reduce.8
  219.7 41.8 all-reduce.10
  314.5 74.6 reduce-scatter.3
  393.3 72.4 reduce-scatter.5
  469.2 39.8 all-reduce.14
  524.4 62.0 reduce-scatter.7
  589.2 94.2 all-reduce.12
where the time goes:
time: 700 us; the launch traced here: 698 us
  waiting for transfers between devices  499 us (71%)
  matrix products  54.2 us (8%)
  local copies, waits for them, and re-layouts  54.1 us (8%)
  blocking collectives  44.7 us (6%)
  other arithmetic  30.3 us (4%)
  between operations  15.2 us (2%)
    psum x1, waiting for transfers between devices, on_device(): packed = lax.psum(packed, 'context')  94.9 us
    reduce_scatter x1, waiting for transfers between devices, on_device(): lax.psum_scatter(back_result[2].astype(jnp.bfloat16), 'context', scatter_...  74.7 us
    reduce_scatter x1, waiting for transfers between devices, on_device(): lax.psum_scatter(back_result[1].astype(jnp.bfloat16), 'context', scatter_...  67.5 us
    reduce_scatter x1, waiting for transfers between devices, on_device(): packed = lax.psum_scatter(packed, 'fsdp', scatter_dimension=0, tiled=True)  62.2 us
    all_gather x1, waiting for transfers between devices, on_device(): lax.all_gather(value_flat, 'context', axis=0, tiled=True)  42.2 us
    psum x1, waiting for transfers between devices, on_device(): lax.psum(jnp.dot(gate_up_grad, gelu_flat.T, preferred_element_type=jnp.fl...  41.8 us
    psum x1, waiting for transfers between devices, on_device(): residual = inputs + lax.psum(attn_part, 'tensor')  40.8 us
    all_gather x1, waiting for transfers between devices, on_device(): lax.all_gather(key_flat, 'context', axis=0, tiled=True)  33.9 us
  transfers between devices with their start and end apart: 11, of which 11 were waited for; matrix products, arithmetic and copies ran while one was open for 7% of the time, Pallas kernels for 0%

commit v1 on v0

--- a/solution.py
+++ b/solution.py
@@ -7,6 +7,24 @@
 EPSILON = 1e-05
 THETA = 160000.0
 MASKED_LOW = -1e30
+
+
+def gather_around(shard, axis, dim):
+    ways, here, step = (lax.axis_size(axis), lax.axis_index(axis), shard.shape[dim])
+    shape = [n * ways if d == dim else n for d, n in enumerate(shard.shape)]
+    full = lax.dynamic_update_slice_in_dim(
+        jnp.zeros(shape, shard.dtype), shard, here * step, axis=dim
+    )
+    going_up = going_down = shard
+    for far in range(1, ways // 2 + 1):
+        going_up = lax.ppermute(going_up, axis, [(d, (d + 1) % ways) for d in range(ways)])
+        full = lax.dynamic_update_slice_in_dim(full, going_up, (here - far) % ways * step, axis=dim)
+        if 2 * far < ways:
+            going_down = lax.ppermute(going_down, axis, [(d, (d - 1) % ways) for d in range(ways)])
+            full = lax.dynamic_update_slice_in_dim(
+                full, going_down, (here + far) % ways * step, axis=dim
+            )
+    return full
 
 
 def layer_norm(values):
@@ -118,7 +136,7 @@
         lax.all_gather(qkv_weight, "fsdp", axis=0, tiled=True),
         lax.all_gather(proj_weight, "fsdp", axis=1, tiled=True),
         lax.all_gather(gelu_weight, "fsdp", axis=0, tiled=True),
-        lax.all_gather(down_weight, "fsdp", axis=1, tiled=True),
+        gather_around(down_weight, "fsdp", 1),
         lax.all_gather(attn_gain, "fsdp", axis=0, tiled=True),
         lax.all_gather(mlp_gain, "fsdp", axis=0, tiled=True),
     )

time: 700 us -> 700 us (level)
  blocking collectives: 44.7 us -> 27.9 us
  starting transfers between devices: 0.67 us -> 9.74 us
    all_gather x1 -> x0, blocking collectives: 16.8 us -> none  [on_device(): lax.all_gather(down_weight, 'fsdp', axis=1, tiled=True)]
    ppermute x0 -> x7, waiting for transfers between devices: none -> 11.5 us  [the longest x4 11.5 us: gather_around(): lax.ppermute(going_up, axis, [(d, (d + 1) % ways) for d in range(ways)])]
    ppermute x0 -> x7, starting transfers between devices: none -> 8.89 us  [the longest x3 8.25 us: gather_around(): lax.ppermute(going_down, axis, [(d, (d - 1) % ways) for d in range(ways)])]
  transfers between devices with their start and end apart: 11 -> 18, of which waited for: 11 -> 13; matrix products, arithmetic and copies ran while one was open for 7% -> 7% of each run, Pallas kernels for 0% -> 0%
where the time goes in v1:
time: 700 us; the launch traced here: 699 us
  waiting for transfers between devices  505 us (72%)
  local copies, waits for them, and re-layouts  56.1 us (8%)
  matrix products  54 us (8%)
  other arithmetic  30.3 us (4%)
  blocking collectives  27.9 us (4%)
  between operations  15.3 us (2%)
  starting transfers between devices  9.74 us (1%)
    psum x1, waiting for transfers between devices, on_device(): packed = lax.psum(packed, 'context')  94.9 us
    reduce_scatter x1, waiting for transfers between devices, on_device(): lax.psum_scatter(back_result[2].astype(jnp.bfloat16), 'context', scatter_...  74.8 us
    reduce_scatter x1, waiting for transfers between devices, on_device(): lax.psum_scatter(back_result[1].astype(jnp.bfloat16), 'context', scatter_...  67.6 us
    reduce_scatter x1, waiting for transfers between devices, on_device(): packed = lax.psum_scatter(packed, 'fsdp', scatter_dimension=0, tiled=True)  62.2 us
    all_gather x1, waiting for transfers between devices, on_device(): lax.all_gather(value_flat, 'context', axis=0, tiled=True)  42.2 us
    psum x1, waiting for transfers between devices, on_device(): lax.psum(jnp.dot(gate_up_grad, gelu_flat.T, preferred_element_type=jnp.fl...  41.8 us
    psum x1, waiting for transfers between devices, on_device(): residual = inputs + lax.psum(attn_part, 'tensor')  41.2 us
    psum x1, waiting for transfers between devices, on_device(): lax.psum(mlp_part.astype(jnp.bfloat16), 'tensor').astype(jnp.float32)  32.8 us
  transfers between devices with their start and end apart: 18, of which 13 were waited for; matrix products, arithmetic and copies ran while one was open for 7% of the time, Pallas kernels for 0%

profile of v1, /device:TPU:0, one launch (start us, length us, event | category | flops | bytes accessed | tf_op | source)
XLA Modules:
  0.0 698.9 jit_solution(6228193635920748750)
XLA Ops:
  11.6 14.7 %all-reduce.2 = (bf16[768]{0:T(1024)(128)(2,1)S(1)}, bf16[768]{0:T(1024)(128)(2,1)S(1)}) all-reduce(bf16[768]{0:T(1024)(128)(2,1)S(1)} %dynamic-update-slice, bf16[768]{0:T(1024)(128)(2,1)S(1)} %dynamic-update-slice.1), channel_id=1, replica_groups=mesh['fsdp'=8,'tensor'=2,'context'=8] {'fsdp'}, use_global_device_ids=true, to_apply=%add | all-reduce | flops 1536 | bytes 6144
  30.6 6.5 all-gather.5.cloned.1.call-done
  48.6 13.2 %all_gather.27 = bf16[384,768]{0,1:T(8,128)(2,1)S(1)} all-gather(bf16[384,96]{0,1:T(8,128)(2,1)S(1)} %copy-done.47), channel_id=1, replica_groups=mesh['fsdp'=8,'tensor'=2,'context'=8] {'fsdp'}, dimensions={1}, use_global_device_ids=true | all-gather | bytes 663552 | tf_op jit(solution)/shard_map/all_gather | solution.py:137
  64.9 27.8 %all-gather.9.cloned.1.call-done = bf16[2048,384]{0,1:T(8,128)(2,1)} async-done(((bf16[256,384]{0,1:T(8,128)(2,1)}), bf16[2048,384]{0,1:T(8,128)(2,1)}) %all-gather.9.cloned.1.call-update) | async-done | bytes 1572880 | tf_op jit(solution)/shard_map/all_gather | solution.py:162
  92.7 3.9 select_reduce_fusion.1
  96.6 3.9 select_reduce_fusion
  101.1 42.2 %all-gather.7.cloned.1.call-done = bf16[2048,384]{0,1:T(8,128)(2,1)} async-done(((bf16[256,384]{0,1:T(8,128)(2,1)}), bf16[2048,384]{0,1:T(8,128)(2,1)}) %all-gather.7.cloned.1.call-update) | async-done | bytes 1572880 | tf_op jit(solution)/shard_map/all_gather | solution.py:163
  143.3 7.6 %fusion.13 = bf16[6,64,256]{2,1,0:T(8,128)(2,1)S(1)} fusion(bf16[2048,6,64]{0,2,1:T(8,128)(2,1)} %bitcast.188, f32[6,256,2048]{2,1,0:T(8,128)} %copy-done.7, f32[6,256]{1,0:T(8,128)S(1)} %log_add_fusion, pred[256,2048]{1,0:T(8,128)(4,1)S(1)} %broadcast_compare_fusion.1), kind=kOutput, calls=%fused_computation.38 | convolution fusion | flops 415334400 | bytes 14882816 | tf_op jit(solution)/shard_map/hqk,khd->qhd/dot_general | solution.py:180
  155.6 4.9 collective-permute-done.4
  160.5 6.6 collective-permute-done.6
  171.9 41.2 %all-reduce.9.cloned.1.call-done = f32[256,768]{1,0:T(8,128)} async-done(((f32[256,768]{1,0:T(8,128)}), f32[256,768]{1,0:T(8,128)}) %all-reduce.9.cloned.1.call-update) | async-done | bytes 786448 | tf_op jit(solution)/shard_map/psum | solution.py:185
  220.1 41.8 %all-reduce.11.cloned.1.call-done = f32[256,768]{1,0:T(8,128)} async-done(((f32[256,768]{1,0:T(8,128)}), f32[256,768]{1,0:T(8,128)}) %all-reduce.11.cloned.1.call-update) | async-done | bytes 786448 | tf_op jit(solution)/shard_map/psum | solution.py:209
  270.8 40.4 %while.20 = (s32[]{:T(128)}, f32[256,6,64]{0,2,1:T(8,128)}, f32[2048,384]{0,1:T(8,128)}, f32[2048,384]{0,1:T(8,128)}, bf16[2048,384]{0,1:T(8,128)(2,1)}, /*index...) while((s32[]{:T(128)}, f32[256,6,64]{0,2,1:T(8,128)}, ...), condition=%wide.region_19.20_spmd.clone, body=%wide.region_17.19_spmd.clone.sunk | while | flops 1024107520 | bytes 131182336 | solution.py:102
  275.3 3.3 fusion.105
  281.3 4.3 fusion.107
  295.5 3.3 fusion.105
  301.5 4.3 fusion.107
  311.2 3.4 convert_element_type.160
  321.9 67.6 %reduce-scatter.4.cloned.1.call-done = bf16[256,384]{0,1:T(8,128)(2,1)} async-done(((bf16[2048,384]{0,1:T(8,128)(2,1)}), bf16[256,384]{0,1:T(8,128)(2,1)}) %reduce-scatter.4.cloned.1.call-update) | async-done | bytes 196624 | tf_op jit(solution)/shard_map/reduce_scatter | solution.py:296
  391.4 74.8 %reduce-scatter.6.cloned.1.call-done = bf16[256,384]{0,1:T(8,128)(2,1)} async-done(((bf16[2048,384]{0,1:T(8,128)(2,1)}), bf16[256,384]{0,1:T(8,128)(2,1)}) %reduce-scatter.6.cloned.1.call-update) | async-done | bytes 196624 | tf_op jit(solution)/shard_map/reduce_scatter | solution.py:299
  476.8 32.8 %all-reduce.15.cloned.1.call-done = (bf16[256,768]{1,0:T(8,128)(2,1)}, bf16[256,768]{1,0:T(8,128)(2,1)}) async-done(((bf16[256,768]{1,0:T(8,128)(2,1)}, bf16[256,768]{1,0:T(8,128)(2,1)}), (bf16[256,768]{1,0:T(8,128)(2,1)}, bf16[256,768]{1,0:T(8,128)(2,1)})) %all-reduce.15.cloned.1.call-update) | async-done | bytes 786448 | tf_op jit(solution)/shard_map/psum | solution.py:197
  511.2 13.5 %concatenate.21 = f32[768,3266]{1,0:T(8,128)} concatenate(f32[768,1]{1,0:T(8,128)S(1)} %broadcast_in_dim.145, f32[768,1]{1,0:T(8,128)S(1)} %broadcast_in_dim.146, f32[768,1152]{1,0:T(8,128)} %fusion.45, f32[768,1152]{1,0:T(8,128)} %fusion.48, f32[768,384]{1,0:T(8,128)} %fusion.38, f32[768,576]{1,0:T(8,128)} %convolution_bitcast_fusion), dimensions={1} | concatenate | bytes 20066304 | tf_op jit(solution)/shard_map/concatenate | solution.py:335
  524.8 62.2 %reduce-scatter.8.cloned.1.call-done = f32[96,3266]{1,0:T(8,128)} async-done(((f32[768,3266]{1,0:T(8,128)}), f32[96,3266]{1,0:T(8,128)}) %reduce-scatter.8.cloned.1.call-update) | async-done | bytes 1254160 | tf_op jit(solution)/shard_map/reduce_scatter | solution.py:336
  589.0 94.9 %all-reduce.13.cloned.1.call-done = f32[96,3266]{1,0:T(8,128)} async-done(((f32[96,3266]{1,0:T(8,128)}), f32[96,3266]{1,0:T(8,128)}) %all-reduce.13.cloned.1.call-update) | async-done | bytes 1254160 | tf_op jit(solution)/shard_map/psum | solution.py:337
  (296 shorter events, 104.6 us)
Async XLA Ops:
  7.2 29.9 %all-gather.5.cloned.1.call-start = ((), (), s32[]{:S(2)}) async-start(), calls=%async_computation.3 | async-start | bytes 1990656 | tf_op jit(solution)/shard_map/all_gather | solution.py:136
  7.9 84.8 %all-gather.9.cloned.1.call-start = ((), (), s32[]{:S(2)}) async-start(), calls=%async_computation.5 | async-start | bytes 1769472 | tf_op jit(solution)/shard_map/all_gather | solution.py:162
  41.8 54.8 %copy-start.34 = (bf16[256,6,32]{0,2,1:T(8,128)(2,1)}, bf16[256,6,32]{0,2,1:T(8,128)(2,1)S(1)}, u32[]{:S(2)}) copy-start(bf16[256,6,32]{0,2,1:T(8,128)(2,1)S(1)} %get-tuple-element.409) | copy-start | bytes 294916
  42.5 100.8 %all-gather.7.cloned.1.call-start = ((), (), s32[]{:S(2)}) async-start(), calls=%async_computation.4 | async-start | bytes 1769472 | tf_op jit(solution)/shard_map/all_gather | solution.py:163
  44.3 124.9 %all-gather.11.cloned.1.call-start = ((), (), s32[]{:S(2)}) async-start(), calls=%async_computation.7 | async-start | bytes 2211840 | tf_op jit(solution)/shard_map/all_gather | solution.py:138
  44.4 17.6 %collective-permute-start = (bf16[576,96]{0,1:T(8,128)(2,1)S(1)}, bf16[576,96]{0,1:T(8,128)(2,1)S(1)}, u32[]{:S(2)}, u32[]{:S(2)}) collective-permute-start(bf16[576,96]{0,1:T(8,128)(2,1)S(1)} %copy-done.46), channel_id=1, source_target_pairs={{0,16},{16,32},{32,48},{48,64},{64,80},{80,96},{96,112},{112,0},{1... | collective-permute-start | bytes 331784 | tf_op jit(solution)/shard_map/ppermute | solution.py:20
  44.6 17.7 %collective-permute-start.1 = (bf16[576,96]{0,1:T(8,128)(2,1)S(1)}, bf16[576,96]{0,1:T(8,128)(2,1)S(1)}, u32[]{:S(2)}, u32[]{:S(2)}) collective-permute-start(bf16[576,96]{0,1:T(8,128)(2,1)S(1)} %copy-done.46), channel_id=1, source_target_pairs={{0,112},{16,0},{32,16},{48,32},{64,48},{80,64},{96,80},{112,96},{1... | collective-permute-start | bytes 331784 | tf_op jit(solution)/shard_map/ppermute | solution.py:23
  48.1 165.0 %all-reduce.9.cloned.1.call-start = ((), (), s32[]{:S(2)}) async-start(), calls=%async_computation.6 | async-start | bytes 1572864 | tf_op jit(solution)/shard_map/psum | solution.py:185
  61.8 89.1 %copy-start.19 = (bf16[384,768]{0,1:T(8,128)(2,1)}, bf16[384,768]{0,1:T(8,128)(2,1)S(1)}, u32[]{:S(2)}) copy-start(bf16[384,768]{0,1:T(8,128)(2,1)S(1)} %all_gather.27) | copy-start | bytes 1769476
  61.9 90.6 %collective-permute-start.2 = (bf16[576,96]{0,1:T(8,128)(2,1)S(1)}, bf16[576,96]{0,1:T(8,128)(2,1)S(1)}, u32[]{:S(2)}, u32[]{:S(2)}) collective-permute-start(bf16[576,96]{0,1:T(8,128)(2,1)S(1)} %collective-permute-done), channel_id=1, source_target_pairs={{0,16},{16,32},{32,48},{48,64},{64,80},{80,96},{96,112},{112,0},{1... | collective-permute-start | bytes 331784 | tf_op jit(solution)/shard_map/ppermute | solution.py:20
  62.3 90.3 %collective-permute-start.3 = (bf16[576,96]{0,1:T(8,128)(2,1)S(1)}, bf16[576,96]{0,1:T(8,128)(2,1)S(1)}, u32[]{:S(2)}, u32[]{:S(2)}) collective-permute-start(bf16[576,96]{0,1:T(8,128)(2,1)S(1)} %collective-permute-done.1), channel_id=1, source_target_pairs={{0,112},{16,0},{32,16},{48,32},{64,48},{80,64},{96,80},{112,96},{1... | collective-permute-start | bytes 331784 | tf_op jit(solution)/shard_map/ppermute | solution.py:23
  152.2 109.6 %all-reduce.11.cloned.1.call-start = ((), (), s32[]{:S(2)}) async-start(), calls=%async_computation.8 | async-start | bytes 1572864 | tf_op jit(solution)/shard_map/psum | solution.py:209
  152.5 7.9 %collective-permute-start.4 = (bf16[576,96]{0,1:T(8,128)(2,1)S(1)}, bf16[576,96]{0,1:T(8,128)(2,1)S(1)}, u32[]{:S(2)}, u32[]{:S(2)}) collective-permute-start(bf16[576,96]{0,1:T(8,128)(2,1)S(1)} %collective-permute-done.2), channel_id=1, source_target_pairs={{0,16},{16,32},{32,48},{48,64},{64,80},{80,96},{96,112},{112,0},{1... | collective-permute-start | bytes 331784 | tf_op jit(solution)/shard_map/ppermute | solution.py:20
  152.6 7.9 %collective-permute-start.5 = (bf16[576,96]{0,1:T(8,128)(2,1)S(1)}, bf16[576,96]{0,1:T(8,128)(2,1)S(1)}, u32[]{:S(2)}, u32[]{:S(2)}) collective-permute-start(bf16[576,96]{0,1:T(8,128)(2,1)S(1)} %collective-permute-done.3), channel_id=1, source_target_pairs={{0,112},{16,0},{32,16},{48,32},{64,48},{80,64},{96,80},{112,96},{1... | collective-permute-start | bytes 331784 | tf_op jit(solution)/shard_map/ppermute | solution.py:23
  160.5 6.6 collective-permute-start.6
  219.8 169.7 %reduce-scatter.4.cloned.1.call-start = ((), (), s32[]{:S(2)}) async-start(), calls=%async_computation.9 | async-start | bytes 1769472 | tf_op jit(solution)/shard_map/reduce_scatter | solution.py:296
  314.7 151.5 %reduce-scatter.6.cloned.1.call-start = ((), (), s32[]{:S(2)}) async-start(), calls=%async_computation.10 | async-start | bytes 1769472 | tf_op jit(solution)/shard_map/reduce_scatter | solution.py:299
  316.2 193.4 %all-reduce.15.cloned.1.call-start = ((), (), s32[]{:S(2)}) async-start(), calls=%async_computation.13 | async-start | bytes 1572864 | tf_op jit(solution)/shard_map/psum | solution.py:197
  319.2 71.3 %copy-start.14 = (f32[256,6,64]{0,2,1:T(8,128)S(1)}, f32[256,6,64]{0,2,1:T(8,128)}, u32[]{:S(2)}) copy-start(f32[256,6,64]{0,2,1:T(8,128)} %get-tuple-element.285) | copy-start | bytes 1179652
  319.2 148.8 %copy-start.13 = (bf16[768,3,384]{0,2,1:T(8,128)(2,1)S(1)}, bf16[768,3,384]{0,2,1:T(8,128)(2,1)}, u32[]{:S(2)}) copy-start(bf16[768,3,384]{0,2,1:T(8,128)(2,1)} %copy-done.12) | copy-start | bytes 5308420
  469.5 117.5 %reduce-scatter.8.cloned.1.call-start = ((), (), s32[]{:S(2)}) async-start(), calls=%async_computation.11 | async-start | bytes 11501568 | tf_op jit(solution)/shard_map/reduce_scatter | solution.py:336
  524.7 62.3 %copy-start.40 = (bf16[256,768]{1,0:T(8,128)(2,1)S(1)}, bf16[256,768]{1,0:T(8,128)(2,1)}, u32[]{:S(2)}) copy-start(bf16[256,768]{1,0:T(8,128)(2,1)} %get-tuple-element.393) | copy-start | bytes 1179652
  524.7 63.2 %copy-start.31 = (bf16[256,768]{1,0:T(8,128)(2,1)S(1)}, bf16[256,768]{1,0:T(8,128)(2,1)}, u32[]{:S(2)}) copy-start(bf16[256,768]{1,0:T(8,128)(2,1)} %get-tuple-element.394) | copy-start | bytes 1179652
  524.7 159.2 %all-reduce.13.cloned.1.call-start = ((), (), s32[]{:S(2)}) async-start(), calls=%async_computation.12 | async-start | bytes 2555904 | tf_op jit(solution)/shard_map/psum | solution.py:337
  (73 other events, 721.7 us)
Sparse Core Ops, SparseCore 0:
  9.7 27.3 all-gather.4
  42.7 50.0 all-gather.8
  95.5 47.7 all-gather.6
  145.4 23.7 all-gather.10
  172.1 40.9 all-reduce.8
  219.9 41.9 all-reduce.10
  314.8 74.6 reduce-scatter.3
  393.7 72.4 reduce-scatter.5
  469.6 39.9 all-reduce.14
  524.9 62.0 reduce-scatter.7
  589.7 94.2 all-reduce.12
